TPU v7x, 32 devices: a whole 2x2x4 slice. The times are simulated.
32 devices in a mesh: grp: 2 (over y), wide: 8 (over z, x), narrow: 2 (over core).
Axes of the slice: x: 2, y: 2, z: 4, core: 2. Of those that a mesh axis runs over, the one named last changes fastest.
Arguments:
- denoised: float32 [4, 512, 512], P('grp', 'wide', 'narrow'), parts along dimension 0, may hold values from -6 to 6
- clean_volume: float32 [4, 512, 512], P('grp', 'wide', 'narrow'), parts along dimension 0, may hold values from -6 to 6
- weight: float32 [512, 512], P(('wide', 'narrow')), may hold values from 0.1 to 2
- act_in: bfloat16 [64, 4, 512, 512], P(None, 'grp', 'wide', 'narrow'), parts along dimension 1, may hold values from -6 to 6
- act_mid: bfloat16 [64, 4, 512, 512], P(None, 'grp', 'wide', 'narrow'), parts along dimension 1, as said below
- w_first: bfloat16 [27, 64, 64], replicated, may hold values from -0.15625 to 0.15625
- w_second: bfloat16 [27, 64], replicated, may hold values from -0.15625 to 0.15625
Outputs:
- grad_in: bfloat16 [64, 4, 512, 512], P(None, 'grp', 'wide', 'narrow'), parts along dimension 1
- grad_first: float32 [54, 64, 64], P('grp'), parts along dimension 0
- grad_second: float32 [54, 64], P('grp'), parts along dimension 0
There are 2 independent parts, one for each index of `grp`. A program takes and returns all parts, laid end to end along the dimension named above; an argument that names none is the same for every part. Nothing has to cross between parts.
Inputs may be any that keep to these rules, and one draw needn't show every extreme that they name: act_mid is a rectifier's output: non-negative, with many zeros.
All inputs are finite; a program needn't handle non-finite values.
Results may differ from a plain program's by a relative error of at most 0.0058.
Values may be sent and summed in bfloat16 or wider, within the bound.
No kernel may reach another device: no remote copies, remote signals or barrier semaphores. Data moves between devices by JAX's collectives and lax.ppermute only.
A program may use at most 320 MiB of HBM per device.

v0:
```python
import jax
import jax.numpy as jnp
from jax import lax
from jax.sharding import PartitionSpec as P

two_pi = 6.283185307179586
highest = lax.Precision.HIGHEST


def with_halo(x, sides, width):
    for axis, dim in sides:
        devices, length = (lax.axis_size(axis), x.shape[dim])
        up = [(i, (i + 1) % devices) for i in range(devices - 1)]
        down = [(j, i) for i, j in up]
        last = lax.slice_in_dim(x, length - width, length, axis=dim)
        first = lax.slice_in_dim(x, 0, width, axis=dim)
        before = lax.ppermute(last, axis, up)
        after = lax.ppermute(first, axis, down)
        x = jnp.concatenate([before, x, after], axis=dim)
    return x


def phase_table(left_index, right_index, length):
    product = left_index[:, None] * right_index[None, :] % length
    angles = product.astype(jnp.float32) * (two_pi / length)
    return (jnp.cos(angles), jnp.sin(angles))


def shifted_windows(padded, slices, rows_x, cols_y, taps_list):
    windows = []
    for tap_index in taps_list:
        step_z = tap_index // 9 - 1
        step_x = tap_index // 3 % 3 - 1
        step_y = tap_index % 3 - 1
        windows.append(
            padded[
                ...,
                1 - step_z : 1 - step_z + slices,
                1 - step_x : 1 - step_x + rows_x,
                1 - step_y : 1 - step_y + cols_y,
            ]
        )
    return jnp.stack(windows, axis=0)


def shards(denoised, clean_volume, weight, act_in, act_mid, w_first, w_second):
    wide_count = lax.axis_size("wide")
    narrow_count = lax.axis_size("narrow")
    slices, rows_x, half_cols = denoised.shape
    total_y = half_cols * narrow_count
    total_x = rows_x * wide_count
    kept_cols = half_cols // wide_count
    narrow_index = lax.axis_index("narrow")
    error_field = denoised - clean_volume
    columns = lax.iota(jnp.int32, total_y)
    frequency = (
        columns % half_cols // kept_cols * narrow_count + columns // half_cols
    ) * kept_cols + columns % kept_cols
    own_rows = narrow_index * half_cols + lax.iota(jnp.int32, half_cols)
    cos_y, sin_y = phase_table(own_rows, frequency, total_y)
    part_real = jnp.einsum("zxy,yc->zxc", error_field, cos_y, precision=highest)
    part_imag = -jnp.einsum("zxy,yc->zxc", error_field, sin_y, precision=highest)
    spec_real, spec_imag = (
        lax.psum_scatter(part_real, "narrow", scatter_dimension=2, tiled=True),
        lax.psum_scatter(part_imag, "narrow", scatter_dimension=2, tiled=True),
    )
    positions = lax.iota(jnp.int32, total_x)
    cos_x, sin_x = phase_table(positions, positions, total_x)
    pieces = (
        lax.all_to_all(
            spec_real.reshape(slices, rows_x, wide_count, kept_cols),
            "wide",
            split_axis=2,
            concat_axis=1,
            tiled=True,
        ),
        lax.all_to_all(
            spec_imag.reshape(slices, rows_x, wide_count, kept_cols),
            "wide",
            split_axis=2,
            concat_axis=1,
            tiled=True,
        ),
    )
    item_count = pieces[0].shape[0]
    in_real = pieces[0].reshape(item_count, total_x, kept_cols)
    in_imag = pieces[1].reshape(item_count, total_x, kept_cols)
    four_real = jnp.einsum("mxk,xq->mkq", in_real, cos_x, precision=highest) + jnp.einsum(
        "mxk,xq->mkq", in_imag, sin_x, precision=highest
    )
    four_imag = jnp.einsum("mxk,xq->mkq", in_imag, cos_x, precision=highest) - jnp.einsum(
        "mxk,xq->mkq", in_real, sin_x, precision=highest
    )
    weighted_real = weight * four_real
    weighted_imag = weight * four_imag
    out_real = jnp.einsum("mkq,qx->mxk", weighted_real, cos_x, precision=highest) - jnp.einsum(
        "mkq,qx->mxk", weighted_imag, sin_x, precision=highest
    )
    out_imag = jnp.einsum("mkq,qx->mxk", weighted_imag, cos_x, precision=highest) + jnp.einsum(
        "mkq,qx->mxk", weighted_real, sin_x, precision=highest
    )
    back_real = lax.all_to_all(
        out_real.reshape(item_count, wide_count, rows_x, kept_cols),
        "wide",
        split_axis=1,
        concat_axis=3,
        tiled=True,
    ).reshape(item_count, rows_x, half_cols)
    back_imag = lax.all_to_all(
        out_imag.reshape(item_count, wide_count, rows_x, kept_cols),
        "wide",
        split_axis=1,
        concat_axis=3,
        tiled=True,
    ).reshape(item_count, rows_x, half_cols)
    local_cols = lax.iota(jnp.int32, half_cols)
    own_freq = (
        local_cols // kept_cols * narrow_count + narrow_index
    ) * kept_cols + local_cols % kept_cols
    cos_back, sin_back = phase_table(own_freq, columns, total_y)
    part_term = jnp.einsum("zxc,cy->zxy", back_real, cos_back, precision=highest) - jnp.einsum(
        "zxc,cy->zxy", back_imag, sin_back, precision=highest
    )
    field_real = lax.psum_scatter(part_term, "narrow", scatter_dimension=2, tiled=True)
    grad_noise = (field_real * (-2.0 / (total_x * total_y))).astype(jnp.bfloat16)
    noise_rim = with_halo(grad_noise, (("wide", 1), ("narrow", 2)), 1)
    noise_pad = jnp.pad(noise_rim, ((1, 1), (0, 0), (0, 0)))
    noise_windows = shifted_windows(noise_pad, slices, rows_x, half_cols, range(27))
    grad_mid = jnp.einsum(
        "tc,tzxy->czxy", w_second, noise_windows, preferred_element_type=jnp.float32
    )
    masked = jnp.where(act_mid > 0, grad_mid, 0.0).astype(jnp.bfloat16)
    masked_rim = with_halo(masked, (("wide", 2), ("narrow", 3)), 1)
    grad_second = jnp.einsum(
        "czxy,tzxy->tc", act_mid, noise_windows, preferred_element_type=jnp.float32
    )
    masked_pad = jnp.pad(masked_rim, ((0, 0), (1, 1), (0, 0), (0, 0)))
    channels = act_in.shape[0]
    grad_in = jnp.zeros(act_in.shape, jnp.float32)
    first_parts = []
    for plane_index in range(9):
        stacked = shifted_windows(
            masked_pad, slices, rows_x, half_cols, [plane_index, plane_index + 9, plane_index + 18]
        )
        first_parts.append(
            jnp.einsum("izxy,dozxy->dio", act_in, stacked, preferred_element_type=jnp.float32)
        )
        grad_in = grad_in + jnp.einsum(
            "dio,dozxy->izxy", w_first[plane_index::9], stacked, preferred_element_type=jnp.float32
        )
    grad_first = jnp.stack(first_parts, axis=1).reshape(27, channels, channels)
    grad_first, grad_second = lax.psum((grad_first, grad_second), ("wide", "narrow"))
    return (grad_in.astype(jnp.bfloat16), grad_first, grad_second)


def solution(mesh):
    placed = (
        P("grp", "wide", "narrow"),
        P("grp", "wide", "narrow"),
        P(("wide", "narrow"), None),
        P(None, "grp", "wide", "narrow"),
        P(None, "grp", "wide", "narrow"),
        P(),
        P(),
    )
    return jax.shard_map(
        shards,
        mesh=mesh,
        in_specs=placed,
        out_specs=(P(None, "grp", "wide", "narrow"), P("grp", None, None), P("grp", None)),
        check_vma=False,
    )
```

profile of v0, /device:TPU:0, one launch (start us, length us, event | category | flops | bytes accessed | tf_op | source)
XLA Modules:
  0.0 590.2 jit_solution(6544291308981167660)
XLA Ops:
  15.5 6.4 %reduce-scatter.4.cloned.1.call-done = f32[2,64,256]{2,1,0:T(8,128)} async-done(((f32[2,64,512]{2,1,0:T(8,128)}), f32[2,64,256]{2,1,0:T(8,128)}) %reduce-scatter.4.cloned.1.call-update) | async-done | bytes 131088 | tf_op jit(solution)/shard_map/reduce_scatter | solution.py:64
  23.8 5.7 all-to-all-start
  98.9 6.0 %all-to-all-done.3 = f32[8,1,4096]{2,1,0:T(1,128)S(1)} async-done(((f32[8,1,4096]{2,1,0:T(1,128)}), f32[8,1,4096]{2,1,0:T(1,128)S(1)}, u32[]{:S(2)}, u32[]{:S(2)}) %all-to-all-start.3) | async-done | bytes 131104 | tf_op jit(solution)/shard_map/all_to_all | solution.py:109
  147.6 6.3 %fusion.100 = f32[27,64]{1,0:T(8,128)S(1)} fusion(bf16[64,2,64,256]{3,2,1,0:T(8,128)(2,1)S(1)} %copy-done.27, bf16[27,2,64,256]{3,2,1,0:T(8,128)(2,1)S(1)} %constant_dynamic-update-slice_fusion), kind=kOutput, calls=%fused_computation.124 | convolution fusion | flops 113246208 | bytes 5970688 | tf_op jit(solution)/shard_map/czxy,tzxy->tc/dot_general | solution.py:134
  154.0 60.0 %psum.15 = f32[27,64]{1,0:T(8,128)} all-reduce(f32[27,64]{1,0:T(8,128)S(1)} %fusion.100), channel_id=1, replica_groups=mesh['grp'=2,'wide'=8,'narrow'=2] {'wide','narrow'}, use_global_device_ids=true, to_apply=%region_4.5 | all-reduce | flops 1728 | bytes 13824 | tf_op jit(solution)/shard_map/psum | solution.py:152
  227.9 5.8 fusion.27
  242.7 8.2 %pad_maximum_fusion.9 = (bf16[64,2,66,257]{3,0,2,1:T(8,128)(2,1)S(1)}, bf16[64,2,66,257]{3,0,2,1:T(8,128)(2,1)S(1)}) fusion(bf16[64,2,66,1]{3,0,2,1:T(8,128)(2,1)} %copy.104, bf16[64,2,1,256]{3,0,2,1:T(8,128)(2,1)S(1)} %collective-permute-done.5, bf16[64,2,64,256]{3,0,2,1:T(8,128)(2,1)} %copy-done.2, bf16[64,2,1,256]{3,0,2,1:T(8,128)(2,1)S(1)} %collective-permute-done.4, ...), kind=kLoop, calls=%fused_computation.30 | loop fusion | flops 34738176 | bytes 13043712 | tf_op jit(solution)/shard_map/concatenate | solution.py:19
  250.9 9.2 %slice_bitcast_fusion.22 = (bf16[1,64,2,64,256]{4,1,3,2,0:T(8,128)(2,1)}, bf16[1,64,2,64,256]{4,1,3,2,0:T(8,128)(2,1)}, bf16[1,64,2,64,256]{4,1,3,2,0:T(8,128)(2,1)}) fusion(bf16[64,2,66,257]{3,0,2,1:T(8,128)(2,1)S(1)} %get-tuple-element.36), kind=kLoop, calls=%fused_computation.77 | loop fusion | bytes 25165824 | tf_op jit(solution)/shard_map/stack | solution.py:43
  260.1 8.9 %select_maximum_fusion = bf16[64,4,66,258]{3,0,2,1:T(8,128)(2,1)} fusion(bf16[64,2,66,1]{3,0,2,1:T(8,128)(2,1)} %copy.104, bf16[64,2,66,1]{3,0,2,1:T(8,128)(2,1)S(1)} %copy-done.4, bf16[64,2,1,256]{3,0,2,1:T(8,128)(2,1)S(1)} %collective-permute-done.5, bf16[64,2,64,256]{3,0,2,1:T(8,128)(2,1)S(1)} %copy-done.3, ...), kind=kLoop, calls=%fused_computation.3 | loop fusion | flops 78465024 | bytes 13077504 | tf_op jit(solution)/shard_map/concatenate | solution.py:19
  269.1 64.1 %slice_bitcast_fusion.23 = (bf16[1,64,2,64,256]{4,1,3,2,0:T(8,128)(2,1)}, bf16[1,64,2,64,256]{4,1,3,2,0:T(8,128)(2,1)}, bf16[1,64,2,64,256]{4,1,3,2,0:T(8,128)(2...) fusion(bf16[64,4,66,258]{3,0,2,1:T(8,128)(2,1)} %select_maximum, ...), kind=kLoop, calls=%fused_computation.78 | loop fusion | bytes 150994944 | tf_op jit(solution)/shard_map/stack | solution.py:43
  333.2 15.3 %fusion.49 = f32[3,9,64,64]{2,3,0,1:T(8,128)} fusion(bf16[1,64,2,64,256]{4,1,3,2,0:T(8,128)(2,1)} %get-tuple-element.28, bf16[1,64,2,64,256]{4,1,3,2,0:T(8,128)(2,1)} %get-tuple-element.30, bf16[1,64,2,64,256]{4,1,3,2,0:T(8,128)(2,1)} %get-tuple-element.12, bf16[64,2,64,256,1]{3,2,1,0,4:T(8,128)(2,1)} %bitcast.559), kind=kOutput, calls=%fused_computation.107 | convolution fusion | flops 817889280 | bytes 16875520 | tf_op jit(solution)/shard_map/izxy,dozxy->dio/dot_general | solution.py:146
  348.6 8.5 %fusion.25 = f32[2,64,256,64,1]{2,3,1,0,4:T(8,128)} fusion(bf16[1,64,2,64,256]{4,1,3,2,0:T(8,128)(2,1)} %get-tuple-element.28, bf16[1,64,2,64,256]{4,1,3,2,0:T(8,128)(2,1)} %get-tuple-element.30, bf16[1,64,2,64,256]{4,1,3,2,0:T(8,128)(2,1)} %get-tuple-element.12, bf16[27,64,64]{2,1,0:T(8,128)(2,1)S(1)} %copy-done.29), kind=kOutput, calls=%fused_computation.49 | convolution fusion | flops 843055104 | bytes 21020672 | tf_op jit(solution)/shard_map/dio,dozxy->izxy/dot_general | solution.py:148
  365.0 9.2 %fusion.55 = f32[3,9,64,64]{2,3,0,1:T(8,128)} fusion(f32[3,9,64,64]{2,3,0,1:T(8,128)} %fusion.49, bf16[1,64,2,64,256]{4,1,3,2,0:T(8,128)(2,1)S(1)} %copy-done.21, bf16[1,64,2,64,256]{4,1,3,2,0:T(8,128)(2,1)S(1)} %copy-done.10, bf16[1,64,2,64,256]{4,1,3,2,0:T(8,128)(2,1)S(1)} %copy-done.22, bf16[64,2,64,256,1]{3,2,1,0,4:T(8,128)(2,1)} %bitcast.560), kind=kOutput, calls=%fused_computation.109 | convolution fusion | flops 817889280 | bytes 16875520 | tf_op jit(solution)/shard_map/izxy,dozxy->dio/dot_general | solution.py:146
  387.2 10.4 %fusion.61 = f32[3,9,64,64]{2,3,0,1:T(8,128)} fusion(f32[3,9,64,64]{2,3,0,1:T(8,128)} %fusion.55, bf16[1,64,2,64,256]{4,1,3,2,0:T(8,128)(2,1)S(1)} %copy-done.19, bf16[1,64,2,64,256]{4,1,3,2,0:T(8,128)(2,1)} %copy-done.26, bf16[1,64,2,64,256]{4,1,3,2,0:T(8,128)(2,1)S(1)} %copy-done.20, bf16[64,2,64,256,1]{3,2,1,0,4:T(8,128)(2,1)} %bitcast.561), kind=kOutput, calls=%fused_computation.111 | convolution fusion | flops 817889280 | bytes 16875520 | tf_op jit(solution)/shard_map/izxy,dozxy->dio/dot_general | solution.py:146
  397.6 6.5 %fusion.19 = f32[2,64,256,64,1]{2,3,1,0,4:T(8,128)} fusion(bf16[1,64,2,64,256]{4,1,3,2,0:T(8,128)(2,1)S(1)} %copy-done.17, bf16[1,64,2,64,256]{4,1,3,2,0:T(8,128)(2,1)} %get-tuple-element.32, bf16[1,64,2,64,256]{4,1,3,2,0:T(8,128)(2,1)S(1)} %copy-done.18, bf16[27,64,64]{2,1,0:T(8,128)(2,1)S(1)} %copy-done.29), kind=kOutput, calls=%fused_computation.43 | convolution fusion | flops 843055104 | bytes 21020672 | tf_op jit(solution)/shard_map/dio,dozxy->izxy/dot_general | solution.py:148
  404.2 10.4 %fusion.67 = f32[3,9,64,64]{2,3,0,1:T(8,128)} fusion(f32[3,9,64,64]{2,3,0,1:T(8,128)} %fusion.61, bf16[1,64,2,64,256]{4,1,3,2,0:T(8,128)(2,1)S(1)} %copy-done.17, bf16[1,64,2,64,256]{4,1,3,2,0:T(8,128)(2,1)} %get-tuple-element.32, bf16[1,64,2,64,256]{4,1,3,2,0:T(8,128)(2,1)S(1)} %copy-done.18, bf16[64,2,64,256,1]{3,2,1,0,4:T(8,128)(2,1)} %bitcast.562), kind=kOutput, calls=%fused_computation.113 | convolution fusion | flops 817889280 | bytes 16875520 | tf_op jit(solution)/shard_map/izxy,dozxy->dio/dot_general | solution.py:146
  420.0 9.3 %fusion.73 = f32[3,9,64,64]{2,3,0,1:T(8,128)} fusion(f32[3,9,64,64]{2,3,0,1:T(8,128)} %fusion.67, bf16[1,64,2,64,256]{4,1,3,2,0:T(8,128)(2,1)S(1)} %copy-done.15, bf16[1,64,2,64,256]{4,1,3,2,0:T(8,128)(2,1)S(1)} %bitcast.549, bf16[1,64,2,64,256]{4,1,3,2,0:T(8,128)(2,1)S(1)} %copy-done.16, bf16[64,2,64,256,1]{3,2,1,0,4:T(8,128)(2,1)} %bitcast.563), kind=kOutput, calls=%fused_computation.115 | convolution fusion | flops 817889280 | bytes 16875520 | tf_op jit(solution)/shard_map/izxy,dozxy->dio/dot_general | solution.py:146
  429.3 6.6 %fusion.15 = f32[2,64,256,64,1]{2,3,1,0,4:T(8,128)} fusion(bf16[1,64,2,64,256]{4,1,3,2,0:T(8,128)(2,1)S(1)} %copy-done.13, bf16[1,64,2,64,256]{4,1,3,2,0:T(8,128)(2,1)} %get-tuple-element.35, bf16[1,64,2,64,256]{4,1,3,2,0:T(8,128)(2,1)S(1)} %copy-done.14, bf16[27,64,64]{2,1,0:T(8,128)(2,1)S(1)} %copy-done.29), kind=kOutput, calls=%fused_computation.39 | convolution fusion | flops 843055104 | bytes 21020672 | tf_op jit(solution)/shard_map/dio,dozxy->izxy/dot_general | solution.py:148
  436.0 10.4 %fusion.79 = f32[3,9,64,64]{2,3,0,1:T(8,128)} fusion(f32[3,9,64,64]{2,3,0,1:T(8,128)} %fusion.73, bf16[1,64,2,64,256]{4,1,3,2,0:T(8,128)(2,1)S(1)} %copy-done.13, bf16[1,64,2,64,256]{4,1,3,2,0:T(8,128)(2,1)} %get-tuple-element.35, bf16[1,64,2,64,256]{4,1,3,2,0:T(8,128)(2,1)S(1)} %copy-done.14, bf16[64,2,64,256,1]{3,2,1,0,4:T(8,128)(2,1)} %bitcast.564), kind=kOutput, calls=%fused_computation.117 | convolution fusion | flops 817889280 | bytes 16875520 | tf_op jit(solution)/shard_map/izxy,dozxy->dio/dot_general | solution.py:146
  451.8 9.3 %fusion.85 = f32[3,9,64,64]{2,3,0,1:T(8,128)} fusion(f32[3,9,64,64]{2,3,0,1:T(8,128)} %fusion.79, bf16[1,64,2,64,256]{4,1,3,2,0:T(8,128)(2,1)S(1)} %copy-done.11, bf16[1,64,2,64,256]{4,1,3,2,0:T(8,128)(2,1)S(1)} %copy-done.24, bf16[1,64,2,64,256]{4,1,3,2,0:T(8,128)(2,1)S(1)} %copy-done.12, bf16[64,2,64,256,1]{3,2,1,0,4:T(8,128)(2,1)} %bitcast.565), kind=kOutput, calls=%fused_computation.119 | convolution fusion | flops 817889280 | bytes 16875520 | tf_op jit(solution)/shard_map/izxy,dozxy->dio/dot_general | solution.py:146
  466.7 9.3 %fusion.91 = f32[3,9,64,64]{2,3,0,1:T(8,128)} fusion(f32[3,9,64,64]{2,3,0,1:T(8,128)} %fusion.85, bf16[1,64,2,64,256]{4,1,3,2,0:T(8,128)(2,1)S(1)} %copy-done.8, bf16[1,64,2,64,256]{4,1,3,2,0:T(8,128)(2,1)S(1)} %copy-done.5, bf16[1,64,2,64,256]{4,1,3,2,0:T(8,128)(2,1)S(1)} %copy-done.9, bf16[64,2,64,256,1]{3,2,1,0,4:T(8,128)(2,1)} %bitcast.566), kind=kOutput, calls=%fused_computation.121 | convolution fusion | flops 817889280 | bytes 16875520 | tf_op jit(solution)/shard_map/izxy,dozxy->dio/dot_general | solution.py:146
  481.3 6.4 %fusion.97 = f32[3,9,64,64]{2,3,0,1:T(8,128)} fusion(f32[3,9,64,64]{2,3,0,1:T(8,128)} %fusion.91, bf16[1,64,2,64,256]{4,1,3,2,0:T(8,128)(2,1)S(1)} %copy-done.7, bf16[1,64,2,64,256]{4,1,3,2,0:T(8,128)(2,1)S(1)} %copy-done.25, bf16[1,64,2,64,256]{4,1,3,2,0:T(8,128)(2,1)S(1)} %copy-done.6, bf16[64,2,64,256,1]{3,2,1,0,4:T(8,128)(2,1)S(1)} %bitcast.567), kind=kOutput, calls=%fused_computation.123 | convolution fusion | flops 817889280 | bytes 16875520 | tf_op jit(solution)/shard_map/izxy,dozxy->dio/dot_general | solution.py:146
  490.1 25.0 %fusion.39 = bf16[64,2,64,256]{3,0,1,2:T(8,128)(2,1)S(1)} fusion(f32[2,64,256,64,1]{2,3,1,0,4:T(8,128)} %fusion.9, f32[2,64,256,64,1]{2,3,1,0,4:T(8,128)} %fusion.11, f32[2,64,256,64,1]{2,3,1,0,4:T(8,128)} %fusion.13, f32[2,64,256,64,1]{2,3,1,0,4:T(8,128)} %fusion.15, f32[2,64,256,64,1]{2,3,1,0,4:T(8,128)} %fusion.17, f32[2,64,256,64,1]{2,3,1,0,4:T(8,128)} %fusion.19, ...), kind=kLoop, calls=%fused_computation.90 | loop fusion | flops 18874368 | bytes 79691776 | tf_op jit(solution)/shard_map/convert_element_type | solution.py:153
  519.6 61.7 %all-reduce.4.cloned.1.call-done = f32[27,64,64]{2,1,0:T(8,128)} async-done(((f32[27,64,64]{2,1,0:T(8,128)}), f32[27,64,64]{2,1,0:T(8,128)}) %all-reduce.4.cloned.1.call-update) | async-done | bytes 442384 | tf_op jit(solution)/shard_map/psum | solution.py:152
  (191 shorter events, 196.1 us)
Async XLA Ops:
  7.2 128.0 %copy-start = (bf16[27,64]{1,0:T(8,128)(2,1)S(1)}, bf16[27,64]{1,0:T(8,128)(2,1)}, u32[]{:S(2)}) copy-start(bf16[27,64]{1,0:T(8,128)(2,1)} %param.13) | copy-start | bytes 10372
  7.2 14.7 %reduce-scatter.4.cloned.1.call-start = ((), (), s32[]{:S(2)}) async-start(), calls=%async_computation.7 | async-start | bytes 393216 | tf_op jit(solution)/shard_map/reduce_scatter | solution.py:64
  11.4 22.3 %reduce-scatter.6.cloned.1.call-start = ((), (), s32[]{:S(2)}) async-start(), calls=%async_computation.8 | async-start | bytes 393216 | tf_op jit(solution)/shard_map/reduce_scatter | solution.py:65
  23.8 13.2 %all-to-all-start = ((f32[8,1,4096]{2,1,0:T(1,128)}), f32[8,1,4096]{2,1,0:T(1,128)S(1)}, u32[]{:S(2)}, u32[]{:S(2)}) async-start(f32[8,1,4096]{2,1,0:T(1,128)} %reshape.165), calls=%async_computation.1 | async-start | bytes 262144 | tf_op jit(solution)/shard_map/all_to_all | solution.py:70
  37.0 12.2 %all-to-all-start.1 = ((f32[8,1,4096]{2,1,0:T(1,128)}), f32[8,1,4096]{2,1,0:T(1,128)S(1)}, u32[]{:S(2)}, u32[]{:S(2)}) async-start(f32[8,1,4096]{2,1,0:T(1,128)} %reshape.167), calls=%async_computation.3 | async-start | bytes 262144 | tf_op jit(solution)/shard_map/all_to_all | solution.py:77
  80.5 12.6 %all-to-all-start.2 = ((f32[8,1,4096]{2,1,0:T(1,128)}), f32[8,1,4096]{2,1,0:T(1,128)S(1)}, u32[]{:S(2)}, u32[]{:S(2)}) async-start(f32[8,1,4096]{2,1,0:T(1,128)} %reshape.169), calls=%async_computation.4 | async-start | bytes 262144 | tf_op jit(solution)/shard_map/all_to_all | solution.py:102
  93.1 11.8 %all-to-all-start.3 = ((f32[8,1,4096]{2,1,0:T(1,128)}), f32[8,1,4096]{2,1,0:T(1,128)S(1)}, u32[]{:S(2)}, u32[]{:S(2)}) async-start(f32[8,1,4096]{2,1,0:T(1,128)} %reshape.171), calls=%async_computation.5 | async-start | bytes 262144 | tf_op jit(solution)/shard_map/all_to_all | solution.py:109
  97.5 19.8 %reduce-scatter.8.cloned.1.call-start = ((), (), s32[]{:S(2)}) async-start(), calls=%async_computation.9 | async-start | bytes 393216 | tf_op jit(solution)/shard_map/reduce_scatter | solution.py:124
  111.7 469.5 %all-reduce.4.cloned.1.call-start = ((), (), s32[]{:S(2)}) async-start(), calls=%async_computation.10 | async-start | bytes 1769472 | tf_op jit(solution)/shard_map/psum | solution.py:152
  117.3 17.8 %copy-start.27 = (bf16[64,2,64,256]{3,2,1,0:T(8,128)(2,1)S(1)}, bf16[64,2,64,256]{3,2,1,0:T(8,128)(2,1)}, u32[]{:S(2)}) copy-start(bf16[64,2,64,256]{3,2,1,0:T(8,128)(2,1)} %param.11) | copy-start | bytes 12582916
  118.4 5.1 collective-permute-start
  122.2 5.5 collective-permute-start.1
  127.8 2.6 collective-permute-start.2
  129.1 3.1 collective-permute-start.3
  141.7 72.4 %collective-permute-start.4 = (bf16[64,2,1,256]{3,0,2,1:T(8,128)(2,1)S(1)}, bf16[64,2,1,256]{3,0,2,1:T(8,128)(2,1)S(1)}, u32[]{:S(2)}, u32[]{:S(2)}) collective-permute-start(bf16[64,2,1,256]{3,0,2,1:T(8,128)(2,1)S(1)} %get-tuple-element.42), channel_id=1, source_target_pairs={{0,2},{2,4},{4,6},{6,8},{8,10},{10,12},{12,14},{1,3},{3,5},{5,7},{... | collective-permute-start | bytes 196616 | tf_op jit(solution)/shard_map/ppermute | solution.py:17
  145.9 68.1 %collective-permute-start.5 = (bf16[64,2,1,256]{3,0,2,1:T(8,128)(2,1)S(1)}, bf16[64,2,1,256]{3,0,2,1:T(8,128)(2,1)S(1)}, u32[]{:S(2)}, u32[]{:S(2)}) collective-permute-start(bf16[64,2,1,256]{3,0,2,1:T(8,128)(2,1)S(1)} %get-tuple-element.43), channel_id=1, source_target_pairs={{2,0},{4,2},{6,4},{8,6},{10,8},{12,10},{14,12},{3,1},{5,3},{7,5},{... | collective-permute-start | bytes 196616 | tf_op jit(solution)/shard_map/ppermute | solution.py:18
  222.6 11.1 %collective-permute-start.6 = (bf16[64,2,66,1]{2,0,3,1:T(8,128)(2,1)S(1)}, bf16[64,2,66,1]{2,0,3,1:T(8,128)(2,1)S(1)}, u32[]{:S(2)}, u32[]{:S(2)}) collective-permute-start(bf16[64,2,66,1]{2,0,3,1:T(8,128)(2,1)S(1)} %copy.101), channel_id=1, source_target_pairs={{0,1},{2,3},{4,5},{6,7},{8,9},{10,11},{12,13},{14,15},{16,17},{18,... | collective-permute-start | bytes 50696 | tf_op jit(solution)/shard_map/ppermute | solution.py:17
  226.4 11.8 %collective-permute-start.7 = (bf16[64,2,66,1]{2,0,3,1:T(8,128)(2,1)S(1)}, bf16[64,2,66,1]{2,0,3,1:T(8,128)(2,1)S(1)}, u32[]{:S(2)}, u32[]{:S(2)}) collective-permute-start(bf16[64,2,66,1]{2,0,3,1:T(8,128)(2,1)S(1)} %copy.102), channel_id=1, source_target_pairs={{1,0},{3,2},{5,4},{7,6},{9,8},{11,10},{13,12},{15,14},{17,16},{19,... | collective-permute-start | bytes 50696 | tf_op jit(solution)/shard_map/ppermute | solution.py:18
  333.2 15.4 %copy-start.29 = (bf16[27,64,64]{2,1,0:T(8,128)(2,1)S(1)}, bf16[27,64,64]{2,1,0:T(8,128)(2,1)}, u32[]{:S(2)}) copy-start(bf16[27,64,64]{2,1,0:T(8,128)(2,1)} %param.12) | copy-start | bytes 663556
  348.6 11.2 %copy-start.22 = (bf16[1,64,2,64,256]{4,1,3,2,0:T(8,128)(2,1)S(1)}, bf16[1,64,2,64,256]{4,1,3,2,0:T(8,128)(2,1)}, u32[]{:S(2)}) copy-start(bf16[1,64,2,64,256]{4,1,3,2,0:T(8,128)(2,1)} %get-tuple-element.27) | copy-start | bytes 12582916
  404.2 10.4 %copy-start.15 = (bf16[1,64,2,64,256]{4,1,3,2,0:T(8,128)(2,1)S(1)}, bf16[1,64,2,64,256]{4,1,3,2,0:T(8,128)(2,1)}, u32[]{:S(2)}) copy-start(bf16[1,64,2,64,256]{4,1,3,2,0:T(8,128)(2,1)} %get-tuple-element.20) | copy-start | bytes 12582916
  435.9 10.5 %copy-start.11 = (bf16[1,64,2,64,256]{4,1,3,2,0:T(8,128)(2,1)S(1)}, bf16[1,64,2,64,256]{4,1,3,2,0:T(8,128)(2,1)}, u32[]{:S(2)}) copy-start(bf16[1,64,2,64,256]{4,1,3,2,0:T(8,128)(2,1)} %get-tuple-element.16) | copy-start | bytes 12582916
  436.0 10.4 %copy-start.12 = (bf16[1,64,2,64,256]{4,1,3,2,0:T(8,128)(2,1)S(1)}, bf16[1,64,2,64,256]{4,1,3,2,0:T(8,128)(2,1)}, u32[]{:S(2)}) copy-start(bf16[1,64,2,64,256]{4,1,3,2,0:T(8,128)(2,1)} %get-tuple-element.17) | copy-start | bytes 12582916
  490.1 93.3 %copy-start.1 = (bf16[27,64]{1,0:T(8,128)(2,1)S(1)}, bf16[27,64]{1,0:T(8,128)(2,1)}, u32[]{:S(2)}) copy-start(bf16[27,64]{1,0:T(8,128)(2,1)} %param.13) | copy-start | bytes 10372
  (23 other events, 189.6 us)
Sparse Core Ops, SparseCore 0:
  11.5 10.3 reduce-scatter.3
  24.8 8.8 reduce-scatter.5
  111.9 5.4 reduce-scatter.7
  490.3 90.9 all-reduce.3
where the time goes:
time: 596 us; the launch traced here: 590 us
  matrix products  207 us (35%)
  local copies, waits for them, and re-layouts  121 us (20%)
  waiting for transfers between devices  93.5 us (16%)
  blocking collectives  60 us (10%)
  other arithmetic  56.7 us (10%)
  starting transfers between devices  36.9 us (6%)
  between operations  14.8 us (2%)
    dot_general x9, matrix products, shards(): jnp.einsum('izxy,dozxy->dio', act_in, stacked, preferred_element_type=jnp...  90.2 us
    another operation x4, local copies, waits for them, and re-layouts, shifted_windows(): return jnp.stack(windows, axis=0)  78.2 us
    psum x1, waiting for transfers between devices, shards(): lax.psum((grad_first, grad_second), ('wide', 'narrow'))  61.7 us
    psum x1, blocking collectives, shards(): lax.psum((grad_first, grad_second), ('wide', 'narrow'))  60 us
    dot_general x9, matrix products, shards(): jnp.einsum('dio,dozxy->izxy', w_first[plane_index::9], stacked, preferred...  53.7 us
    convert_element_type x1, other arithmetic, shards(): return (grad_in.astype(jnp.bfloat16), grad_first, grad_second)  25 us
    concatenate x6, other arithmetic, with_halo(): x = jnp.concatenate([before, x, after], axis=dim)  19.9 us
    unnamed x95, local copies, waits for them, and re-layouts  19.5 us
  transfers between devices with their start and end apart: 16, of which 10 were waited for; matrix products, arithmetic and copies ran while one was open for 12% of the time, Pallas kernels for 0%

commit v1 on v0

--- a/solution.py
+++ b/solution.py
@@ -149,7 +149,7 @@
             "dio,dozxy->izxy", w_first[plane_index::9], stacked, preferred_element_type=jnp.float32
         )
     grad_first = jnp.stack(first_parts, axis=1).reshape(27, channels, channels)
-    grad_first, grad_second = lax.psum((grad_first, grad_second), ("wide", "narrow"))
+    grad_first, grad_second = lax.psum(lax.psum((grad_first, grad_second), "wide"), "narrow")
     return (grad_in.astype(jnp.bfloat16), grad_first, grad_second)
 
 

time: 596 us -> 591 us (level)
  blocking collectives: 60 us -> 39.8 us
  matrix products: 207 us -> 216 us
    psum x1 -> x2, blocking collectives: 60 us -> 39.8 us  [the longest x1 35.9 us: shards(): lax.psum((grad_first, grad_second), 'wide')]
    psum x1 -> x2, waiting for transfers between devices: 61.7 us -> 65.6 us  [the longest x1 65.6 us: shards(): lax.psum((grad_first, grad_second), 'wide')]
  transfers between devices with their start and end apart: 16 -> 17, of which waited for: 10 -> 10; matrix products, arithmetic and copies ran while one was open for 12% -> 13% of each run, Pallas kernels for 0% -> 0%
where the time goes in v1:
time: 591 us; the launch traced here: 586 us
  matrix products  216 us (37%)
  local copies, waits for them, and re-layouts  122 us (21%)
  waiting for transfers between devices  97.5 us (16%)
  other arithmetic  57.2 us (10%)
  blocking collectives  39.8 us (7%)
  starting transfers between devices  37.8 us (6%)
  between operations  14.9 us (3%)
    dot_general x9, matrix products, shards(): jnp.einsum('izxy,dozxy->dio', act_in, stacked, preferred_element_type=jnp...  96.1 us
    another operation x4, local copies, waits for them, and re-layouts, shifted_windows(): return jnp.stack(windows, axis=0)  78.2 us
    psum x1, waiting for transfers between devices, shards(): lax.psum((grad_first, grad_second), 'wide')  65.6 us
    dot_general x9, matrix products, shards(): jnp.einsum('dio,dozxy->izxy', w_first[plane_index::9], stacked, preferred...  56.6 us
    psum x1, blocking collectives, shards(): lax.psum((grad_first, grad_second), 'wide')  35.9 us
    convert_element_type x1, other arithmetic, shards(): return (grad_in.astype(jnp.bfloat16), grad_first, grad_second)  25.6 us
    unnamed x95, local copies, waits for them, and re-layouts  20.2 us
    concatenate x6, other arithmetic, with_halo(): x = jnp.concatenate([before, x, after], axis=dim)  19.9 us
  transfers between devices with their start and end apart: 17, of which 10 were waited for; matrix products, arithmetic and copies ran while one was open for 13% of the time, Pallas kernels for 0%

profile of v1, /device:TPU:0, one launch (start us, length us, event | category | flops | bytes accessed | tf_op | source)
XLA Modules:
  0.0 585.6 jit_solution(13320713795234896540)
XLA Ops:
  15.5 6.4 %reduce-scatter.4.cloned.1.call-done = f32[2,64,256]{2,1,0:T(8,128)} async-done(((f32[2,64,512]{2,1,0:T(8,128)}), f32[2,64,256]{2,1,0:T(8,128)}) %reduce-scatter.4.cloned.1.call-update) | async-done | bytes 131088 | tf_op jit(solution)/shard_map/reduce_scatter | solution.py:64
  99.1 6.0 %all-to-all-done.3 = f32[8,1,4096]{2,1,0:T(1,128)S(1)} async-done(((f32[8,1,4096]{2,1,0:T(1,128)}), f32[8,1,4096]{2,1,0:T(1,128)S(1)}, u32[]{:S(2)}, u32[]{:S(2)}) %all-to-all-start.3) | async-done | bytes 131104 | tf_op jit(solution)/shard_map/all_to_all | solution.py:109
  147.6 6.3 %fusion.100 = f32[27,64]{1,0:T(8,128)S(1)} fusion(bf16[64,2,64,256]{3,2,1,0:T(8,128)(2,1)S(1)} %copy-done.28, bf16[27,2,64,256]{3,2,1,0:T(8,128)(2,1)S(1)} %constant_dynamic-update-slice_fusion), kind=kOutput, calls=%fused_computation.124 | convolution fusion | flops 113246208 | bytes 5970688 | tf_op jit(solution)/shard_map/czxy,tzxy->tc/dot_general | solution.py:134
  154.0 35.9 %psum.30 = f32[27,64]{1,0:T(8,128)S(1)} all-reduce(f32[27,64]{1,0:T(8,128)S(1)} %fusion.100), channel_id=1, replica_groups=mesh['grp'=2,'wide'=8,'narrow'=2] {'wide'}, use_global_device_ids=true, to_apply=%region_5.6 | all-reduce | flops 1728 | bytes 13824 | tf_op jit(solution)/shard_map/psum | solution.py:152
  208.9 5.8 fusion.27
  223.7 8.2 %pad_maximum_fusion.9 = (bf16[64,2,66,257]{3,0,2,1:T(8,128)(2,1)S(1)}, bf16[64,2,66,257]{3,0,2,1:T(8,128)(2,1)S(1)}) fusion(bf16[64,2,66,1]{3,0,2,1:T(8,128)(2,1)} %copy.104, bf16[64,2,1,256]{3,0,2,1:T(8,128)(2,1)S(1)} %collective-permute-done.5, bf16[64,2,64,256]{3,0,2,1:T(8,128)(2,1)} %copy-done.2, bf16[64,2,1,256]{3,0,2,1:T(8,128)(2,1)S(1)} %collective-permute-done.4, ...), kind=kLoop, calls=%fused_computation.30 | loop fusion | flops 34738176 | bytes 13043712 | tf_op jit(solution)/shard_map/concatenate | solution.py:19
  231.9 9.2 %slice_bitcast_fusion.22 = (bf16[1,64,2,64,256]{4,1,3,2,0:T(8,128)(2,1)}, bf16[1,64,2,64,256]{4,1,3,2,0:T(8,128)(2,1)}, bf16[1,64,2,64,256]{4,1,3,2,0:T(8,128)(2,1)}) fusion(bf16[64,2,66,257]{3,0,2,1:T(8,128)(2,1)S(1)} %get-tuple-element.36), kind=kLoop, calls=%fused_computation.77 | loop fusion | bytes 25165824 | tf_op jit(solution)/shard_map/stack | solution.py:43
  241.0 9.0 %select_maximum_fusion = bf16[64,4,66,258]{3,0,2,1:T(8,128)(2,1)} fusion(bf16[64,2,66,1]{3,0,2,1:T(8,128)(2,1)} %copy.104, bf16[64,2,66,1]{3,0,2,1:T(8,128)(2,1)S(1)} %copy-done.4, bf16[64,2,1,256]{3,0,2,1:T(8,128)(2,1)S(1)} %collective-permute-done.5, bf16[64,2,64,256]{3,0,2,1:T(8,128)(2,1)S(1)} %copy-done.3, ...), kind=kLoop, calls=%fused_computation.3 | loop fusion | flops 78465024 | bytes 13077504 | tf_op jit(solution)/shard_map/concatenate | solution.py:19
  250.0 64.1 %slice_bitcast_fusion.23 = (bf16[1,64,2,64,256]{4,1,3,2,0:T(8,128)(2,1)}, bf16[1,64,2,64,256]{4,1,3,2,0:T(8,128)(2,1)}, bf16[1,64,2,64,256]{4,1,3,2,0:T(8,128)(2...) fusion(bf16[64,4,66,258]{3,0,2,1:T(8,128)(2,1)} %select_maximum, ...), kind=kLoop, calls=%fused_computation.78 | loop fusion | bytes 150994944 | tf_op jit(solution)/shard_map/stack | solution.py:43
  314.1 14.6 %fusion.49 = f32[3,9,64,64]{2,3,0,1:T(8,128)S(1)} fusion(bf16[1,64,2,64,256]{4,1,3,2,0:T(8,128)(2,1)} %get-tuple-element.28, bf16[1,64,2,64,256]{4,1,3,2,0:T(8,128)(2,1)} %get-tuple-element.30, bf16[1,64,2,64,256]{4,1,3,2,0:T(8,128)(2,1)} %get-tuple-element.12, bf16[64,2,64,256,1]{3,2,1,0,4:T(8,128)(2,1)} %bitcast.559), kind=kOutput, calls=%fused_computation.107 | convolution fusion | flops 817889280 | bytes 16875520 | tf_op jit(solution)/shard_map/izxy,dozxy->dio/dot_general | solution.py:146
  328.7 8.5 %fusion.25 = f32[2,64,256,64,1]{2,3,1,0,4:T(8,128)} fusion(bf16[1,64,2,64,256]{4,1,3,2,0:T(8,128)(2,1)} %get-tuple-element.28, bf16[1,64,2,64,256]{4,1,3,2,0:T(8,128)(2,1)} %get-tuple-element.30, bf16[1,64,2,64,256]{4,1,3,2,0:T(8,128)(2,1)} %get-tuple-element.12, bf16[27,64,64]{2,1,0:T(8,128)(2,1)S(1)} %copy-done.29), kind=kOutput, calls=%fused_computation.49 | convolution fusion | flops 843055104 | bytes 21020672 | tf_op jit(solution)/shard_map/dio,dozxy->izxy/dot_general | solution.py:148
  345.1 10.0 %fusion.55 = f32[3,9,64,64]{2,3,0,1:T(8,128)S(1)} fusion(f32[3,9,64,64]{2,3,0,1:T(8,128)S(1)} %fusion.49, bf16[1,64,2,64,256]{4,1,3,2,0:T(8,128)(2,1)S(1)} %copy-done.21, bf16[1,64,2,64,256]{4,1,3,2,0:T(8,128)(2,1)S(1)} %copy-done.10, bf16[1,64,2,64,256]{4,1,3,2,0:T(8,128)(2,1)S(1)} %copy-done.22, bf16[64,2,64,256,1]{3,2,1,0,4:T(8,128)(2,1)} %bitcast.560), kind=kOutput, calls=%fused_computation.109 | convolution fusion | flops 817889280 | bytes 16875520 | tf_op jit(solution)/shard_map/izxy,dozxy->dio/dot_general | solution.py:146
  367.9 11.4 %fusion.61 = f32[3,9,64,64]{2,3,0,1:T(8,128)S(1)} fusion(f32[3,9,64,64]{2,3,0,1:T(8,128)S(1)} %fusion.55, bf16[1,64,2,64,256]{4,1,3,2,0:T(8,128)(2,1)S(1)} %copy-done.19, bf16[1,64,2,64,256]{4,1,3,2,0:T(8,128)(2,1)} %copy-done.26, bf16[1,64,2,64,256]{4,1,3,2,0:T(8,128)(2,1)S(1)} %copy-done.20, bf16[64,2,64,256,1]{3,2,1,0,4:T(8,128)(2,1)} %bitcast.561), kind=kOutput, calls=%fused_computation.111 | convolution fusion | flops 817889280 | bytes 16875520 | tf_op jit(solution)/shard_map/izxy,dozxy->dio/dot_general | solution.py:146
  379.3 6.8 %fusion.19 = f32[2,64,256,64,1]{2,3,1,0,4:T(8,128)} fusion(bf16[1,64,2,64,256]{4,1,3,2,0:T(8,128)(2,1)S(1)} %copy-done.17, bf16[1,64,2,64,256]{4,1,3,2,0:T(8,128)(2,1)} %get-tuple-element.32, bf16[1,64,2,64,256]{4,1,3,2,0:T(8,128)(2,1)S(1)} %copy-done.18, bf16[27,64,64]{2,1,0:T(8,128)(2,1)S(1)} %copy-done.29), kind=kOutput, calls=%fused_computation.43 | convolution fusion | flops 843055104 | bytes 21020672 | tf_op jit(solution)/shard_map/dio,dozxy->izxy/dot_general | solution.py:148
  386.1 11.5 %fusion.67 = f32[3,9,64,64]{2,3,0,1:T(8,128)S(1)} fusion(f32[3,9,64,64]{2,3,0,1:T(8,128)S(1)} %fusion.61, bf16[1,64,2,64,256]{4,1,3,2,0:T(8,128)(2,1)S(1)} %copy-done.17, bf16[1,64,2,64,256]{4,1,3,2,0:T(8,128)(2,1)} %get-tuple-element.32, bf16[1,64,2,64,256]{4,1,3,2,0:T(8,128)(2,1)S(1)} %copy-done.18, bf16[64,2,64,256,1]{3,2,1,0,4:T(8,128)(2,1)} %bitcast.562), kind=kOutput, calls=%fused_computation.113 | convolution fusion | flops 817889280 | bytes 16875520 | tf_op jit(solution)/shard_map/izxy,dozxy->dio/dot_general | solution.py:146
  403.0 10.3 %fusion.73 = f32[3,9,64,64]{2,3,0,1:T(8,128)S(1)} fusion(f32[3,9,64,64]{2,3,0,1:T(8,128)S(1)} %fusion.67, bf16[1,64,2,64,256]{4,1,3,2,0:T(8,128)(2,1)S(1)} %copy-done.15, bf16[1,64,2,64,256]{4,1,3,2,0:T(8,128)(2,1)S(1)} %bitcast.549, bf16[1,64,2,64,256]{4,1,3,2,0:T(8,128)(2,1)S(1)} %copy-done.16, bf16[64,2,64,256,1]{3,2,1,0,4:T(8,128)(2,1)} %bitcast.563), kind=kOutput, calls=%fused_computation.115 | convolution fusion | flops 817889280 | bytes 16875520 | tf_op jit(solution)/shard_map/izxy,dozxy->dio/dot_general | solution.py:146
  414.2 6.6 %fusion.15 = f32[2,64,256,64,1]{2,3,1,0,4:T(8,128)} fusion(bf16[1,64,2,64,256]{4,1,3,2,0:T(8,128)(2,1)S(1)} %copy-done.13, bf16[1,64,2,64,256]{4,1,3,2,0:T(8,128)(2,1)} %get-tuple-element.35, bf16[1,64,2,64,256]{4,1,3,2,0:T(8,128)(2,1)S(1)} %copy-done.14, bf16[27,64,64]{2,1,0:T(8,128)(2,1)S(1)} %copy-done.29), kind=kOutput, calls=%fused_computation.39 | convolution fusion | flops 843055104 | bytes 21020672 | tf_op jit(solution)/shard_map/dio,dozxy->izxy/dot_general | solution.py:148
  420.9 10.4 %fusion.79 = f32[3,9,64,64]{2,3,0,1:T(8,128)} fusion(f32[3,9,64,64]{2,3,0,1:T(8,128)} %copy-done.27, bf16[1,64,2,64,256]{4,1,3,2,0:T(8,128)(2,1)S(1)} %copy-done.13, bf16[1,64,2,64,256]{4,1,3,2,0:T(8,128)(2,1)} %get-tuple-element.35, bf16[1,64,2,64,256]{4,1,3,2,0:T(8,128)(2,1)S(1)} %copy-done.14, bf16[64,2,64,256,1]{3,2,1,0,4:T(8,128)(2,1)} %bitcast.564), kind=kOutput, calls=%fused_computation.117 | convolution fusion | flops 817889280 | bytes 16875520 | tf_op jit(solution)/shard_map/izxy,dozxy->dio/dot_general | solution.py:146
  436.6 9.3 %fusion.85 = f32[3,9,64,64]{2,3,0,1:T(8,128)} fusion(f32[3,9,64,64]{2,3,0,1:T(8,128)} %fusion.79, bf16[1,64,2,64,256]{4,1,3,2,0:T(8,128)(2,1)S(1)} %copy-done.11, bf16[1,64,2,64,256]{4,1,3,2,0:T(8,128)(2,1)S(1)} %copy-done.24, bf16[1,64,2,64,256]{4,1,3,2,0:T(8,128)(2,1)S(1)} %copy-done.12, bf16[64,2,64,256,1]{3,2,1,0,4:T(8,128)(2,1)} %bitcast.565), kind=kOutput, calls=%fused_computation.119 | convolution fusion | flops 817889280 | bytes 16875520 | tf_op jit(solution)/shard_map/izxy,dozxy->dio/dot_general | solution.py:146
  451.5 9.3 %fusion.91 = f32[3,9,64,64]{2,3,0,1:T(8,128)} fusion(f32[3,9,64,64]{2,3,0,1:T(8,128)} %fusion.85, bf16[1,64,2,64,256]{4,1,3,2,0:T(8,128)(2,1)S(1)} %copy-done.8, bf16[1,64,2,64,256]{4,1,3,2,0:T(8,128)(2,1)S(1)} %copy-done.5, bf16[1,64,2,64,256]{4,1,3,2,0:T(8,128)(2,1)S(1)} %copy-done.9, bf16[64,2,64,256,1]{3,2,1,0,4:T(8,128)(2,1)} %bitcast.566), kind=kOutput, calls=%fused_computation.121 | convolution fusion | flops 817889280 | bytes 16875520 | tf_op jit(solution)/shard_map/izxy,dozxy->dio/dot_general | solution.py:146
  460.8 9.2 %fusion.97 = f32[3,9,64,64]{2,3,0,1:T(8,128)} fusion(f32[3,9,64,64]{2,3,0,1:T(8,128)} %fusion.91, bf16[1,64,2,64,256]{4,1,3,2,0:T(8,128)(2,1)S(1)} %copy-done.7, bf16[1,64,2,64,256]{4,1,3,2,0:T(8,128)(2,1)S(1)} %copy-done.25, bf16[1,64,2,64,256]{4,1,3,2,0:T(8,128)(2,1)S(1)} %copy-done.6, bf16[64,2,64,256,1]{3,2,1,0,4:T(8,128)(2,1)} %bitcast.567), kind=kOutput, calls=%fused_computation.123 | convolution fusion | flops 817889280 | bytes 16875520 | tf_op jit(solution)/shard_map/izxy,dozxy->dio/dot_general | solution.py:146
  472.6 8.3 %fusion.9 = f32[2,64,256,64,1]{2,3,1,0,4:T(8,128)} fusion(bf16[1,64,2,64,256]{4,1,3,2,0:T(8,128)(2,1)} %get-tuple-element.29, bf16[1,64,2,64,256]{4,1,3,2,0:T(8,128)(2,1)} %get-tuple-element.34, bf16[1,64,2,64,256]{4,1,3,2,0:T(8,128)(2,1)} %get-tuple-element.13, bf16[27,64,64]{2,1,0:T(8,128)(2,1)S(1)} %copy-done.29), kind=kOutput, calls=%fused_computation.33 | convolution fusion | flops 843055104 | bytes 21020672 | tf_op jit(solution)/shard_map/dio,dozxy->izxy/dot_general | solution.py:148
  480.9 65.6 %all-reduce.5.cloned.1.call-done = f32[27,64,64]{2,1,0:T(8,128)} async-done(((f32[27,64,64]{2,1,0:T(8,128)}), f32[27,64,64]{2,1,0:T(8,128)}) %all-reduce.5.cloned.1.call-update) | async-done | bytes 442384 | tf_op jit(solution)/shard_map/psum | solution.py:152
  546.6 25.6 %fusion.39 = bf16[64,2,64,256]{3,0,1,2:T(8,128)(2,1)S(1)} fusion(f32[2,64,256,64,1]{2,3,1,0,4:T(8,128)} %fusion.9, f32[2,64,256,64,1]{2,3,1,0,4:T(8,128)} %fusion.11, f32[2,64,256,64,1]{2,3,1,0,4:T(8,128)} %fusion.13, f32[2,64,256,64,1]{2,3,1,0,4:T(8,128)} %fusion.15, f32[2,64,256,64,1]{2,3,1,0,4:T(8,128)} %fusion.17, f32[2,64,256,64,1]{2,3,1,0,4:T(8,128)} %fusion.19, ...), kind=kLoop, calls=%fused_computation.90 | loop fusion | flops 18874368 | bytes 79691776 | tf_op jit(solution)/shard_map/convert_element_type | solution.py:153
  (195 shorter events, 202.3 us)
Async XLA Ops:
  7.2 128.1 %copy-start = (bf16[27,64]{1,0:T(8,128)(2,1)S(1)}, bf16[27,64]{1,0:T(8,128)(2,1)}, u32[]{:S(2)}) copy-start(bf16[27,64]{1,0:T(8,128)(2,1)} %param.13) | copy-start | bytes 10372
  7.2 14.7 %reduce-scatter.4.cloned.1.call-start = ((), (), s32[]{:S(2)}) async-start(), calls=%async_computation.7 | async-start | bytes 393216 | tf_op jit(solution)/shard_map/reduce_scatter | solution.py:64
  11.4 22.3 %reduce-scatter.6.cloned.1.call-start = ((), (), s32[]{:S(2)}) async-start(), calls=%async_computation.8 | async-start | bytes 393216 | tf_op jit(solution)/shard_map/reduce_scatter | solution.py:65
  23.8 13.2 %all-to-all-start = ((f32[8,1,4096]{2,1,0:T(1,128)}), f32[8,1,4096]{2,1,0:T(1,128)S(1)}, u32[]{:S(2)}, u32[]{:S(2)}) async-start(f32[8,1,4096]{2,1,0:T(1,128)} %reshape.165), calls=%async_computation.1 | async-start | bytes 262144 | tf_op jit(solution)/shard_map/all_to_all | solution.py:70
  37.0 12.0 %all-to-all-start.1 = ((f32[8,1,4096]{2,1,0:T(1,128)}), f32[8,1,4096]{2,1,0:T(1,128)S(1)}, u32[]{:S(2)}, u32[]{:S(2)}) async-start(f32[8,1,4096]{2,1,0:T(1,128)} %reshape.167), calls=%async_computation.3 | async-start | bytes 262144 | tf_op jit(solution)/shard_map/all_to_all | solution.py:77
  80.7 12.6 %all-to-all-start.2 = ((f32[8,1,4096]{2,1,0:T(1,128)}), f32[8,1,4096]{2,1,0:T(1,128)S(1)}, u32[]{:S(2)}, u32[]{:S(2)}) async-start(f32[8,1,4096]{2,1,0:T(1,128)} %reshape.169), calls=%async_computation.4 | async-start | bytes 262144 | tf_op jit(solution)/shard_map/all_to_all | solution.py:102
  93.2 11.8 %all-to-all-start.3 = ((f32[8,1,4096]{2,1,0:T(1,128)}), f32[8,1,4096]{2,1,0:T(1,128)S(1)}, u32[]{:S(2)}, u32[]{:S(2)}) async-start(f32[8,1,4096]{2,1,0:T(1,128)} %reshape.171), calls=%async_computation.5 | async-start | bytes 262144 | tf_op jit(solution)/shard_map/all_to_all | solution.py:109
  97.7 19.8 %reduce-scatter.8.cloned.1.call-start = ((), (), s32[]{:S(2)}) async-start(), calls=%async_computation.9 | async-start | bytes 393216 | tf_op jit(solution)/shard_map/reduce_scatter | solution.py:124
  111.9 434.6 %all-reduce.5.cloned.1.call-start = ((), (), s32[]{:S(2)}) async-start(), calls=%async_computation.10 | async-start | bytes 1769472 | tf_op jit(solution)/shard_map/psum | solution.py:152
  117.5 17.8 %copy-start.28 = (bf16[64,2,64,256]{3,2,1,0:T(8,128)(2,1)S(1)}, bf16[64,2,64,256]{3,2,1,0:T(8,128)(2,1)}, u32[]{:S(2)}) copy-start(bf16[64,2,64,256]{3,2,1,0:T(8,128)(2,1)} %param.11) | copy-start | bytes 12582916
  118.6 5.0 collective-permute-start
  122.4 5.5 collective-permute-start.1
  127.9 2.6 collective-permute-start.2
  129.2 3.1 collective-permute-start.3
  141.8 52.0 %collective-permute-start.4 = (bf16[64,2,1,256]{3,0,2,1:T(8,128)(2,1)S(1)}, bf16[64,2,1,256]{3,0,2,1:T(8,128)(2,1)S(1)}, u32[]{:S(2)}, u32[]{:S(2)}) collective-permute-start(bf16[64,2,1,256]{3,0,2,1:T(8,128)(2,1)S(1)} %get-tuple-element.42), channel_id=1, source_target_pairs={{0,2},{2,4},{4,6},{6,8},{8,10},{10,12},{12,14},{1,3},{3,5},{5,7},{... | collective-permute-start | bytes 196616 | tf_op jit(solution)/shard_map/ppermute | solution.py:17
  146.1 47.7 %collective-permute-start.5 = (bf16[64,2,1,256]{3,0,2,1:T(8,128)(2,1)S(1)}, bf16[64,2,1,256]{3,0,2,1:T(8,128)(2,1)S(1)}, u32[]{:S(2)}, u32[]{:S(2)}) collective-permute-start(bf16[64,2,1,256]{3,0,2,1:T(8,128)(2,1)S(1)} %get-tuple-element.43), channel_id=1, source_target_pairs={{2,0},{4,2},{6,4},{8,6},{10,8},{12,10},{14,12},{3,1},{5,3},{7,5},{... | collective-permute-start | bytes 196616 | tf_op jit(solution)/shard_map/ppermute | solution.py:18
  202.4 12.3 %collective-permute-start.6 = (bf16[64,2,66,1]{2,0,3,1:T(8,128)(2,1)S(1)}, bf16[64,2,66,1]{2,0,3,1:T(8,128)(2,1)S(1)}, u32[]{:S(2)}, u32[]{:S(2)}) collective-permute-start(bf16[64,2,66,1]{2,0,3,1:T(8,128)(2,1)S(1)} %copy.101), channel_id=1, source_target_pairs={{0,1},{2,3},{4,5},{6,7},{8,9},{10,11},{12,13},{14,15},{16,17},{18,... | collective-permute-start | bytes 50696 | tf_op jit(solution)/shard_map/ppermute | solution.py:17
  207.2 12.0 %collective-permute-start.7 = (bf16[64,2,66,1]{2,0,3,1:T(8,128)(2,1)S(1)}, bf16[64,2,66,1]{2,0,3,1:T(8,128)(2,1)S(1)}, u32[]{:S(2)}, u32[]{:S(2)}) collective-permute-start(bf16[64,2,66,1]{2,0,3,1:T(8,128)(2,1)S(1)} %copy.102), channel_id=1, source_target_pairs={{1,0},{3,2},{5,4},{7,6},{9,8},{11,10},{13,12},{15,14},{17,16},{19,... | collective-permute-start | bytes 50696 | tf_op jit(solution)/shard_map/ppermute | solution.py:18
  314.1 14.6 %copy-start.29 = (bf16[27,64,64]{2,1,0:T(8,128)(2,1)S(1)}, bf16[27,64,64]{2,1,0:T(8,128)(2,1)}, u32[]{:S(2)}) copy-start(bf16[27,64,64]{2,1,0:T(8,128)(2,1)} %param.12) | copy-start | bytes 663556
  367.9 11.4 %copy-start.17 = (bf16[1,64,2,64,256]{4,1,3,2,0:T(8,128)(2,1)S(1)}, bf16[1,64,2,64,256]{4,1,3,2,0:T(8,128)(2,1)}, u32[]{:S(2)}) copy-start(bf16[1,64,2,64,256]{4,1,3,2,0:T(8,128)(2,1)} %get-tuple-element.22) | copy-start | bytes 12582916
  386.1 11.5 %copy-start.15 = (bf16[1,64,2,64,256]{4,1,3,2,0:T(8,128)(2,1)S(1)}, bf16[1,64,2,64,256]{4,1,3,2,0:T(8,128)(2,1)}, u32[]{:S(2)}) copy-start(bf16[1,64,2,64,256]{4,1,3,2,0:T(8,128)(2,1)} %get-tuple-element.20) | copy-start | bytes 12582916
  386.1 11.5 %copy-start.16 = (bf16[1,64,2,64,256]{4,1,3,2,0:T(8,128)(2,1)S(1)}, bf16[1,64,2,64,256]{4,1,3,2,0:T(8,128)(2,1)}, u32[]{:S(2)}) copy-start(bf16[1,64,2,64,256]{4,1,3,2,0:T(8,128)(2,1)} %get-tuple-element.21) | copy-start | bytes 12582916
  472.6 104.1 %all-reduce.7.cloned.1.call-start = ((), (), s32[]{:S(2)}) async-start(), calls=%async_computation.11 | async-start | bytes 1769472 | tf_op jit(solution)/shard_map/psum | solution.py:152
  546.6 32.3 %copy-start.1 = (bf16[27,64]{1,0:T(8,128)(2,1)S(1)}, bf16[27,64]{1,0:T(8,128)(2,1)}, u32[]{:S(2)}) copy-start(bf16[27,64]{1,0:T(8,128)(2,1)} %param.13) | copy-start | bytes 10372
  (24 other events, 201.2 us)
Sparse Core Ops, SparseCore 0:
  11.5 10.3 reduce-scatter.3
  24.8 8.8 reduce-scatter.5
  112.0 5.4 reduce-scatter.7
  472.7 73.7 all-reduce.4
  548.9 18.5 all-reduce.6
